TPU v7x, 512 devices: a whole 4x4x16 slice. The times are simulated.
512 devices in a mesh: lon: 128 (over x_lo, z, y), lat: 4 (over x_hi, core).
Axes of the slice: x: 4 (x_hi: 2, x_lo: 2; x = x_hi * 2 + x_lo), y: 4, z: 16, core: 2. Of those that a mesh axis runs over, the one named last changes fastest.
Arguments:
- queries: bfloat16 [64, 2048, 256], P('lat', 'lon'), may hold values from -11 to 11
- key_values: bfloat16 [2, 64, 2048, 256], P(None, 'lat', 'lon'), may hold values from -11 to 11
- pole_mask: int32 [8], replicated, may hold values 0 or 1
- sea_mask: int32 [8, 256], replicated, may hold values 0 or 1
- reg_queries: bfloat16 [256, 256], replicated, may hold values from -21 to 21
- reg_keys: bfloat16 [256, 256], replicated, may hold values from -6 to 6
Outputs:
- attended: bfloat16 [64, 2048, 256], P('lat', 'lon')
- reg_out: bfloat16 [256, 256], replicated
All inputs are finite; a program needn't handle non-finite values.
Results may differ from a plain program's by a relative error of at most 0.0048.
Values may be sent and summed in bfloat16 or wider, within the bound.
A program may use at most 64 MiB of HBM per device.

v0:
```python
import jax
import jax.numpy as jnp
from jax import lax
from jax.sharding import PartitionSpec as P

HEADS = 4
HEAD_DIM = 64
NREG = 256
RADIUS = 6
TILE = 8
QROWS = 16


def extended_2(shard, sides, width):
    for axis, dim in sides:
        peers, length = (lax.axis_size(axis), shard.shape[dim])
        up = [(i, (i + 1) % peers) for i in range(peers)]
        down = [(j, i) for i, j in up]
        last = lax.slice_in_dim(shard, length - width, length, axis=dim)
        leading = lax.slice_in_dim(shard, 0, width, axis=dim)
        before = lax.ppermute(last, axis, up)
        after = lax.ppermute(leading, axis, down)
        shard = jnp.concatenate([before, shard, after], axis=dim)
    return shard


def key_window(pole_mask, sea_mask, lat_first, lon_first, ext_rows, ext_cols, grid_cols):
    lat_cells = lat_first + jnp.arange(ext_rows, dtype=jnp.int32) - RADIUS
    lon_cells = (lon_first + jnp.arange(ext_cols, dtype=jnp.int32) - RADIUS) % grid_cols
    row_pick = (
        lat_cells[:, None] // TILE == jnp.arange(pole_mask.shape[0], dtype=jnp.int32)[None, :]
    ).astype(jnp.float32)
    row_pick = row_pick * pole_mask.astype(jnp.float32)[None, :]
    col_pick = (
        lon_cells[:, None] // TILE == jnp.arange(sea_mask.shape[1], dtype=jnp.int32)[None, :]
    ).astype(jnp.float32)
    coverage = jnp.dot(jnp.dot(row_pick, sea_mask.astype(jnp.float32)), col_pick.T)
    return coverage > 0.5


def register_values(key_values, reg_queries):
    lat_rows, lon_cols, channels = key_values.shape[1:]
    scale_factor = HEAD_DIM ** (-0.5)
    local_keys = key_values[0].reshape(lat_rows * lon_cols, HEADS, HEAD_DIM)
    local_values = key_values[1].reshape(lat_rows * lon_cols, HEADS, HEAD_DIM)
    query_heads = reg_queries.reshape(NREG, HEADS, HEAD_DIM)
    scores = (
        jnp.einsum("rhd,khd->hrk", query_heads, local_keys, preferred_element_type=jnp.float32)
        * scale_factor
    )
    highest = lax.pmax(jnp.max(scores, axis=2), ("lon", "lat"))
    weights = jnp.exp(scores - highest[:, :, None])
    weight_sums = jnp.sum(weights, axis=2).T
    weighted = jnp.einsum(
        "hrk,khd->rhd",
        weights.astype(jnp.bfloat16),
        local_values,
        preferred_element_type=jnp.float32,
    )
    weighted = weighted.reshape(NREG, channels)
    total_sums, total_weighted = lax.psum((weight_sums, weighted), ("lon", "lat"))
    merged = (total_weighted.reshape(NREG, HEADS, HEAD_DIM) / total_sums[:, :, None]).astype(
        jnp.bfloat16
    )
    finished = merged.reshape(NREG, channels)
    return finished


def shards(queries, key_values, pole_mask, sea_mask, reg_queries, reg_keys):
    lat_rows, lon_cols, channels = queries.shape
    scale_factor = HEAD_DIM ** (-0.5)
    ext_rows = lat_rows + 2 * RADIUS
    ext_cols = lon_cols + 2 * RADIUS
    grid_cols = lon_cols * lax.axis_size("lon")
    extended = extended_2(key_values, (("lon", 2), ("lat", 1)), RADIUS)
    reg_vals = register_values(key_values, reg_queries)
    keep_window = key_window(
        pole_mask,
        sea_mask,
        lax.axis_index("lat") * lat_rows,
        lax.axis_index("lon") * lon_cols,
        ext_rows,
        ext_cols,
        grid_cols,
    )
    block_rows = QROWS
    query_count = block_rows * lon_cols
    key_count = (block_rows + 2 * RADIUS) * ext_cols
    query_index = jnp.arange(query_count, dtype=jnp.int32)
    key_index = jnp.arange(key_count, dtype=jnp.int32)
    query_lat = query_index // lon_cols
    query_lon = query_index % lon_cols
    key_lat = key_index // ext_cols
    key_lon = key_index % ext_cols
    nearby = (jnp.abs(key_lat[None, :] - RADIUS - query_lat[:, None]) <= RADIUS) & (
        jnp.abs(key_lon[None, :] - RADIUS - query_lon[:, None]) <= RADIUS
    )
    reg_key_heads = reg_keys.reshape(NREG, HEADS, HEAD_DIM)
    reg_value_heads = reg_vals.reshape(NREG, HEADS, HEAD_DIM)

    def one_block(first_row):
        block_queries = queries.reshape(query_count, HEADS, HEAD_DIM)
        block_keys = extended[0].reshape(key_count, HEADS, HEAD_DIM)
        block_values = extended[1].reshape(key_count, HEADS, HEAD_DIM)
        block_keep = keep_window.reshape(key_count)
        allowed = nearby & block_keep[None, :]
        near_scores = (
            jnp.einsum(
                "qhd,khd->hqk", block_queries, block_keys, preferred_element_type=jnp.float32
            )
            * scale_factor
        )
        near_scores = jnp.where(allowed[None], near_scores, -jnp.inf)
        reg_scores = (
            jnp.einsum(
                "qhd,rhd->hqr", block_queries, reg_key_heads, preferred_element_type=jnp.float32
            )
            * scale_factor
        )
        highest = jnp.maximum(jnp.max(near_scores, axis=2), jnp.max(reg_scores, axis=2))
        near_weights = jnp.exp(near_scores - highest[:, :, None])
        reg_weights = jnp.exp(reg_scores - highest[:, :, None])
        weight_sums = jnp.sum(near_weights, axis=2) + jnp.sum(reg_weights, axis=2)
        mixture = jnp.einsum(
            "hqk,khd->qhd",
            near_weights.astype(jnp.bfloat16),
            block_values,
            preferred_element_type=jnp.float32,
        )
        mixture = mixture + jnp.einsum(
            "hqr,rhd->qhd",
            reg_weights.astype(jnp.bfloat16),
            reg_value_heads,
            preferred_element_type=jnp.float32,
        )
        result = mixture / weight_sums.T[:, :, None]
        return result.astype(jnp.bfloat16).reshape(block_rows, lon_cols, channels)

    starts = jnp.arange(lat_rows // block_rows, dtype=jnp.int32) * block_rows
    blocks = lax.map(one_block, starts)
    return (blocks.reshape(lat_rows, lon_cols, channels), reg_vals)


def solution(mesh):
    return jax.shard_map(
        shards,
        mesh=mesh,
        in_specs=(P("lat", "lon", None), P(None, "lat", "lon", None), P(), P(), P(), P()),
        out_specs=(P("lat", "lon", None), P()),
        check_vma=False,
    )
```

profile of v0, /device:TPU:1, one launch (start us, length us, event | category | flops | bytes accessed | tf_op | source)
XLA Modules:
  0.0 596.8 jit_solution(12302706617695983196)
XLA Ops:
  7.2 1.0 fusion.62
  8.3 4.0 collective-permute-start
  12.3 13.2 %collective-permute-start.1 = (bf16[2,16,6,256]{3,2,1,0:T(8,128)(2,1)S(1)}, bf16[2,16,6,256]{3,2,1,0:T(8,128)(2,1)S(1)}, u32[]{:S(2)}, u32[]{:S(2)}) collective-permute-start(bf16[2,16,6,256]{3,2,1,0:T(8,128)(2,1)S(1)} %get-tuple-element.37), channel_id=1, source_target_pairs={{4,0},{8,4},{12,8},{16,12},{20,16},{24,20},{28,24},{32,28},{36,32}... | collective-permute-start | bytes 294920 | tf_op jit(solution)/shard_map/ppermute | solution.py:22
  25.5 1.0 fusion.61
  26.5 0.2 reshape_squeeze.6
  26.7 1.0 copy.27
  27.7 0.3 fusion.64
  28.0 99.8 %pmax.7 = f32[4,256]{1,0:T(4,128)S(1)} all-reduce(f32[4,256]{1,0:T(4,128)S(1)} %get-tuple-element.42), channel_id=1, replica_groups=mesh['lon'=128,'lat'=4] {'lon','lat'}, use_global_device_ids=true, to_apply=%region_3.0 | all-reduce | flops 1024 | bytes 8192 | tf_op jit(solution)/shard_map/pmax | solution.py:51
  128.0 1.0 fusion.25
  129.0 0.2 fusion.15
  129.2 0.3 fusion.12
  129.8 0.2 copy.23
  130.1 100.0 %psum.15 = f32[256,4]{0,1:T(4,128)S(1)} all-reduce(f32[256,4]{0,1:T(4,128)S(1)} %bitcast.40), channel_id=1, replica_groups=mesh['lon'=128,'lat'=4] {'lon','lat'}, use_global_device_ids=true, to_apply=%region_6.7 | all-reduce | flops 1024 | bytes 8192 | tf_op jit(solution)/shard_map/psum | solution.py:61
  230.1 0.4 fusion.63
  230.5 0.2 pad_maximum_fusion.3
  230.7 3.8 collective-permute-start.2
  234.5 1.9 collective-permute-start.3
  236.4 0.8 fusion.23
  237.2 342.5 %all-reduce.2.cloned.1.call-done = f32[256,256]{0,1:T(8,128)} async-done(((f32[256,256]{0,1:T(8,128)}), f32[256,256]{0,1:T(8,128)}) %all-reduce.2.cloned.1.call-update) | async-done | bytes 262160 | tf_op jit(solution)/shard_map/psum | solution.py:61
  579.6 1.0 fusion.29
  580.6 0.8 copy.33
  581.4 0.3 pad_maximum_fusion
  581.7 0.3 squeeze.9
  582.1 0.7 fusion.2
  582.8 1.6 copy-done.1
  584.4 0.7 fusion
  585.1 0.2 fusion.17
  585.3 0.3 squeeze.8
  585.7 2.9 fusion.3
  588.6 0.3 fusion.8
  588.9 0.2 copy.32
  589.1 0.9 reshape.255
  (30 shorter events, 0.7 us)
Async XLA Ops:
  7.2 122.0 %copy-start.6 = (s32[8]{0:T(128)S(1)}, s32[8]{0:T(128)}, u32[]{:S(2)}) copy-start(s32[8]{0:T(128)} %param.8) | copy-start | bytes 100
  7.2 122.0 %copy-start.5 = (s32[8,256]{1,0:T(8,128)S(1)}, s32[8,256]{1,0:T(8,128)}, u32[]{:S(2)}) copy-start(s32[8,256]{1,0:T(8,128)} %param.9) | copy-start | bytes 24580
  7.2 122.5 %copy-start.3 = (bf16[16,16,256]{2,1,0:T(8,128)(2,1)S(1)}, bf16[16,16,256]{2,1,0:T(8,128)(2,1)}, u32[]{:S(2)}) copy-start(bf16[16,16,256]{2,1,0:T(8,128)(2,1)} %param.6) | copy-start | bytes 393220
  7.2 572.4 %all-reduce.2.cloned.1.call-start = ((), (), s32[]{:S(2)}) async-start(), calls=%async_computation | async-start | bytes 524288 | tf_op jit(solution)/shard_map/psum | solution.py:61
  8.3 222.2 %collective-permute-start = (bf16[2,16,6,256]{3,2,1,0:T(8,128)(2,1)S(1)}, bf16[2,16,6,256]{3,2,1,0:T(8,128)(2,1)S(1)}, u32[]{:S(2)}, u32[]{:S(2)}) collective-permute-start(bf16[2,16,6,256]{3,2,1,0:T(8,128)(2,1)S(1)} %get-tuple-element.36), channel_id=1, source_target_pairs={{0,4},{4,8},{8,12},{12,16},{16,20},{20,24},{24,28},{28,32},{32,36}... | collective-permute-start | bytes 294920 | tf_op jit(solution)/shard_map/ppermute | solution.py:21
  12.3 218.2 %collective-permute-start.1 = (bf16[2,16,6,256]{3,2,1,0:T(8,128)(2,1)S(1)}, bf16[2,16,6,256]{3,2,1,0:T(8,128)(2,1)S(1)}, u32[]{:S(2)}, u32[]{:S(2)}) collective-permute-start(bf16[2,16,6,256]{3,2,1,0:T(8,128)(2,1)S(1)} %get-tuple-element.37), channel_id=1, source_target_pairs={{4,0},{8,4},{12,8},{16,12},{20,16},{24,20},{28,24},{32,28},{36,32}... | collective-permute-start | bytes 294920 | tf_op jit(solution)/shard_map/ppermute | solution.py:22
  26.5 103.5 %copy-start.4 = (bf16[256,256]{1,0:T(8,128)(2,1)S(1)}, bf16[256,256]{1,0:T(8,128)(2,1)}, u32[]{:S(2)}) copy-start(bf16[256,256]{1,0:T(8,128)(2,1)} %param.11) | copy-start | bytes 393220
  28.0 202.5 %copy-start = (bf16[2,16,16,256]{3,2,1,0:T(8,128)(2,1)S(1)}, bf16[2,16,16,256]{3,2,1,0:T(8,128)(2,1)}, u32[]{:S(2)}) copy-start(bf16[2,16,16,256]{3,2,1,0:T(8,128)(2,1)} %param.7) | copy-start | bytes 786436
  230.7 350.7 %collective-permute-start.2 = (bf16[2,6,28,256]{3,2,1,0:T(8,128)(2,1)S(1)}, bf16[2,6,28,256]{3,2,1,0:T(8,128)(2,1)S(1)}, u32[]{:S(2)}, u32[]{:S(2)}) collective-permute-start(bf16[2,6,28,256]{3,2,1,0:T(8,128)(2,1)S(1)} %get-tuple-element.32), channel_id=1, source_target_pairs={{0,1},{1,2},{2,3},{3,0},{4,5},{5,6},{6,7},{7,4},{8,9},{9,10},{10,1... | collective-permute-start | bytes 516104 | tf_op jit(solution)/shard_map/ppermute | solution.py:21
  234.5 346.9 %collective-permute-start.3 = (bf16[2,6,28,256]{3,2,1,0:T(8,128)(2,1)S(1)}, bf16[2,6,28,256]{3,2,1,0:T(8,128)(2,1)S(1)}, u32[]{:S(2)}, u32[]{:S(2)}) collective-permute-start(bf16[2,6,28,256]{3,2,1,0:T(8,128)(2,1)S(1)} %get-tuple-element.33), channel_id=1, source_target_pairs={{1,0},{2,1},{3,2},{0,3},{5,4},{6,5},{7,6},{4,7},{9,8},{10,9},{11,1... | collective-permute-start | bytes 516104 | tf_op jit(solution)/shard_map/ppermute | solution.py:22
  582.8 1.7 copy-start.1
  585.3 3.3 copy-start.2
Sparse Core Ops, SparseCore 0:
  129.1 450.4 all-reduce.1
where the time goes:
time: 598 us; the launch traced here: 597 us
  waiting for transfers between devices  342 us (57%)
  blocking collectives  200 us (33%)
  starting transfers between devices  23 us (4%)
  between operations  14.4 us (2%)
  local copies, waits for them, and re-layouts  8.11 us (1%)
    psum x1, waiting for transfers between devices, register_values(): lax.psum((weight_sums, weighted), ('lon', 'lat'))  342 us
    psum x1, blocking collectives, register_values(): lax.psum((weight_sums, weighted), ('lon', 'lat'))  100 us
    pmax x1, blocking collectives, register_values(): highest = lax.pmax(jnp.max(scores, axis=2), ('lon', 'lat'))  99.8 us
    ppermute x2, starting transfers between devices, extended_2(): after = lax.ppermute(leading, axis, down)  15.1 us
  transfers between devices with their start and end apart: 5, of which 1 were waited for; matrix products, arithmetic and copies ran while one was open for 1% of the time, Pallas kernels for 0%

commit v1 on v0

v1 whole, which is shorter than its diff:
```python
import functools

import jax
import jax.numpy as jnp
from jax import lax
from jax.experimental import pallas as pl
from jax.experimental.pallas import tpu as pltpu
from jax.sharding import PartitionSpec as P

HEADS = 4
HEAD_DIM = 64
NREG = 256
RADIUS = 6
TILE = 8
CHANNELS = 256
ROWS = 16
COLS = 16
CELLS = ROWS * COLS
SIDE = ROWS * TILE
KEYS = 896
LOG2_SCALE = HEAD_DIM ** (-0.5) * 1.4426950408889634
NX, NY, NZ = 4, 4, 16
OWN = 8
WIDE = CHANNELS + 128
MASKED = -1e30
MESH = pl.DeviceIdType.MESH

PLANE = sorted(
    [(c, x, y) for c in range(2) for x in range(NX) for y in range(NY) if (c, x, y) != (0, 0, 0)],
    key=lambda o: -(min(o[1], NX - o[1]) + min(o[2], NY - o[2])),
)
LINE = sorted(range(1, NZ), key=lambda k: -min(k, NZ - k))

PIECES = (
    (256, 128, 0, 1),
    (384, 128, 0, -1),
    (512, 96, -1, 0),
    (608, 96, 1, 0),
    (704, 48, -1, -1),
    (752, 48, -1, 1),
    (800, 48, 1, -1),
    (848, 48, 1, 1),
)


def place():
    lon, lat = lax.axis_index("lon"), lax.axis_index("lat")
    return lat % 2, (lat // 2) * 2 + lon // (NY * NZ), lon % NY, (lon // NY) % NZ


def device(core, x, y, z):
    return {"lon": (x % 2) * (NY * NZ) + z * NY + y, "lat": (x // 2) * 2 + core}


def nt(a, b):
    return lax.dot_general(a, b, (((1,), (1,)), ((), ())), preferred_element_type=jnp.float32)


def nn(a, b):
    return jnp.dot(a, b, preferred_element_type=jnp.float32)


def head_of(rows, lanes=CHANNELS):
    return lax.broadcasted_iota(jnp.int32, (rows, lanes), 1) // HEAD_DIM


def only(head, lanes, x):
    return jnp.where(lanes == head, x.astype(jnp.float32), 0.0).astype(jnp.bfloat16)


def merge(theirs, mine):
    logs, own_log = theirs[:, :, CHANNELS:], mine[:, CHANNELS:]
    top = jnp.maximum(jnp.max(logs, axis=0), own_log)
    part = jnp.exp2(logs - top[None])
    own_part = jnp.exp2(own_log - top)
    total = jnp.sum(part, axis=0) + own_part
    low = lax.broadcasted_iota(jnp.int32, (OWN, 128), 1) < HEAD_DIM

    def spread(x, half):
        return jnp.where(low, x[..., 2 * half : 2 * half + 1], x[..., 2 * half + 1 : 2 * half + 2])

    out = []
    for half in range(2):
        cols = slice(128 * half, 128 * half + 128)
        summed = spread(own_part, half) * mine[:, cols]
        summed = summed + jnp.sum(spread(part, half) * theirs[:, :, cols], axis=0)
        out.append(summed / spread(total, half))
    return out, top + jnp.log2(total)


def kernel(
    pole, sea, q, kv, rq, rk, att, reg_out,
    window, sides, msg1, buf1, msg2, buf2, final, reg_w, near, inverse, bias,
    hs, hr, s1, r1, s2, r2, s3, r3,
):
    core, x, y, z = place()
    lon, lat = lax.axis_index("lon"), lax.axis_index("lat")
    lons, lats = lax.axis_size("lon"), lax.axis_size("lat")
    me = (core * NX + x) * NY + y
    plane = [(lax.rem(core + c, 2), lax.rem(x + a, NX), lax.rem(y + b, NY)) for c, a, b in PLANE]
    plane_ids = [device(c, a, b, z) for c, a, b in plane]
    line_ids = [device(core, x, y, lax.rem(z + k, NZ)) for k in LINE]
    halo_ids = [
        {"lon": lax.rem(lon - b + lons, lons), "lat": lax.rem(lat - a + lats, lats)}
        for _, _, a, b in PIECES
    ]
    barrier = pltpu.get_barrier_semaphore()
    for other in plane_ids + line_ids + halo_ids:
        pl.semaphore_signal(barrier, inc=1, device_id=other, device_id_type=MESH)

    lanes = head_of(NREG)
    stat_lane = lax.broadcasted_iota(jnp.int32, (NREG, 128), 1)
    keys, values = kv[0], kv[1]
    gathered = jnp.zeros((NREG, CHANNELS), jnp.float32)
    logs = jnp.zeros((NREG, 128), jnp.float32)
    for h in range(HEADS):
        scores = nt(only(h, lanes, rq[...]), keys) * LOG2_SCALE
        top = jnp.max(scores, axis=1, keepdims=True)
        weights = jnp.exp2(scores - top)
        total = jnp.sum(weights, axis=1, keepdims=True)
        mixed = nn(weights.astype(jnp.bfloat16), values) / total
        gathered = jnp.where(lanes == h, mixed, gathered)
        logs = jnp.where(stat_lane == h, top + jnp.log2(total), logs)
    msg1[:, :, :CHANNELS] = gathered.reshape(NREG // OWN, OWN, CHANNELS)
    msg1[:, :, CHANNELS:] = logs.reshape(NREG // OWN, OWN, 128)

    for i in range(2):
        window[i, :CELLS] = kv[i]
        split = kv[i].astype(jnp.float32).reshape(ROWS, 2, TILE, CHANNELS)
        for side in range(2):
            sides[side, i] = split[:, side].reshape(SIDE, CHANNELS).astype(jnp.bfloat16)

    pl.semaphore_wait(barrier, len(plane_ids) + len(line_ids) + len(halo_ids))
    for k, (c, a, b) in enumerate(plane):
        pltpu.make_async_remote_copy(
            msg1.at[(c * NX + a) * NY + b], buf1.at[k], s1, r1, device_id=plane_ids[k], device_id_type=MESH
        ).start()
    for k, (first, count, a, b) in enumerate(PIECES):
        if b == 0:
            own = pl.ds(0 if a > 0 else CELLS - count, count)
            source = window.at[:, own]
        else:
            own = pl.ds(0 if a >= 0 else SIDE - count, count)
            source = sides.at[0 if b > 0 else 1, :, own]
        pltpu.make_async_remote_copy(
            source, window.at[:, pl.ds(first, count)], hs, hr, device_id=halo_ids[k], device_id_type=MESH
        ).start()

    spot = lax.broadcasted_iota(jnp.int32, (1, KEYS), 1)
    key_lat = jnp.zeros((1, KEYS), jnp.int32)
    key_lon = jnp.zeros((1, KEYS), jnp.int32)
    for first, count, a, b in ((0, CELLS, 0, 0),) + PIECES:
        width = COLS if b == 0 else TILE
        here = (spot >= first) & (spot < first + count)
        base_lat = 0 if a == 0 else (-RADIUS if a < 0 else ROWS)
        base_lon = 0 if b == 0 else (-TILE if b < 0 else COLS)
        key_lat = jnp.where(here, base_lat + (spot - first) // width, key_lat)
        key_lon = jnp.where(here, base_lon + (spot - first) % width, key_lon)
    tile_lat, tile_lon = (key_lat + TILE) // TILE, (key_lon + TILE) // TILE
    kept = jnp.zeros((1, KEYS), jnp.int32)
    tile_rows, tile_cols = 8, 256
    for a in range(4):
        row = lat * 2 - 1 + a
        inside = jnp.where((row >= 0) & (row < tile_rows), 1, 0)
        row = jnp.clip(row, 0, tile_rows - 1)
        band = pole[row] * inside
        for b in range(4):
            col = lax.rem(lon * 2 - 1 + b + tile_cols, tile_cols)
            kept = jnp.where((tile_lat == a) & (tile_lon == b), band * sea[row, col], kept)
    cell = lax.broadcasted_iota(jnp.int32, (CELLS, 1), 0)
    near_by = (
        (jnp.abs(key_lat - cell // COLS) <= RADIUS)
        & (jnp.abs(key_lon - cell % COLS) <= RADIUS)
        & (kept > 0)
    )
    bias[...] = jnp.where(near_by, 0.0, MASKED)

    pltpu.make_async_copy(buf1, buf1, r1).wait()
    halves, log = merge(buf1[...], msg1[me])
    for half in range(2):
        msg2[:, 128 * half : 128 * half + 128] = halves[half]
    msg2[:, CHANNELS:] = log
    for k, other in enumerate(line_ids):
        pltpu.make_async_remote_copy(
            msg2, buf2.at[k], s2, r2, device_id=other, device_id_type=MESH
        ).start()

    pltpu.make_async_copy(window.at[:, pl.ds(CELLS, KEYS - CELLS)], window.at[:, pl.ds(CELLS, KEYS - CELLS)], hr).wait()
    mixture = jnp.zeros((CELLS, CHANNELS), jnp.float32)
    totals = jnp.zeros((CELLS, CHANNELS), jnp.float32)
    for h in range(HEADS):
        query = only(h, lanes, q[...])
        near_scores = nt(query, window[0]) * LOG2_SCALE + bias[...]
        reg_scores = nt(query, rk[...]) * LOG2_SCALE
        top = jnp.maximum(
            jnp.max(near_scores, axis=1, keepdims=True), jnp.max(reg_scores, axis=1, keepdims=True)
        )
        near_weights = jnp.exp2(near_scores - top)
        reg_weights = jnp.exp2(reg_scores - top)
        total = jnp.sum(near_weights, axis=1, keepdims=True) + jnp.sum(reg_weights, axis=1, keepdims=True)
        reg_w[h] = reg_weights.astype(jnp.bfloat16)
        mixture = jnp.where(lanes == h, nn(near_weights.astype(jnp.bfloat16), window[1]), mixture)
        totals = jnp.where(lanes == h, total, totals)
    near[...] = mixture
    inverse[...] = 1.0 / totals

    pltpu.make_async_copy(buf2, buf2, r2).wait()
    halves, _ = merge(buf2[...], msg2[...])
    for half in range(2):
        final[me, :, 128 * half : 128 * half + 128] = halves[half].astype(jnp.bfloat16)
    for k, other in enumerate(plane_ids):
        pltpu.make_async_remote_copy(
            final.at[me], final.at[me], s3, r3, device_id=other, device_id_type=MESH
        ).start()

    pltpu.make_async_copy(final.at[pl.ds(0, 31)], final.at[pl.ds(0, 31)], r3).wait()
    reg_values = final[...].astype(jnp.float32).reshape(NREG, CHANNELS).astype(jnp.bfloat16)
    reg_out[...] = reg_values
    mixture = jnp.zeros((CELLS, CHANNELS), jnp.float32)
    for h in range(HEADS):
        mixture = jnp.where(lanes == h, nn(reg_w[h], reg_values), mixture)
    att[...] = ((near[...] + mixture) * inverse[...]).astype(jnp.bfloat16)

    pltpu.make_async_copy(buf1, buf1, s1).wait()
    pltpu.make_async_copy(window.at[:, pl.ds(CELLS, KEYS - CELLS)], window.at[:, pl.ds(CELLS, KEYS - CELLS)], hs).wait()
    pltpu.make_async_copy(buf2, buf2, s2).wait()
    pltpu.make_async_copy(final.at[pl.ds(0, 31)], final.at[pl.ds(0, 31)], s3).wait()


def shards(queries, key_values, pole_mask, sea_mask, reg_queries, reg_keys):
    vmem = pl.BlockSpec(memory_space=pltpu.VMEM)
    smem = pl.BlockSpec(memory_space=pltpu.SMEM)
    att, reg_vals = pl.pallas_call(
        kernel,
        out_shape=(
            jax.ShapeDtypeStruct((CELLS, CHANNELS), jnp.bfloat16),
            jax.ShapeDtypeStruct((NREG, CHANNELS), jnp.bfloat16),
        ),
        in_specs=[smem, smem, vmem, vmem, vmem, vmem],
        out_specs=(vmem, vmem),
        scratch_shapes=[
            pltpu.VMEM((2, KEYS, CHANNELS), jnp.bfloat16),
            pltpu.VMEM((2, 2, SIDE, CHANNELS), jnp.bfloat16),
            pltpu.VMEM((32, OWN, WIDE), jnp.float32),
            pltpu.VMEM((31, OWN, WIDE), jnp.float32),
            pltpu.VMEM((OWN, WIDE), jnp.float32),
            pltpu.VMEM((NZ - 1, OWN, WIDE), jnp.float32),
            pltpu.VMEM((32, OWN, CHANNELS), jnp.bfloat16),
            pltpu.VMEM((HEADS, CELLS, NREG), jnp.bfloat16),
            pltpu.VMEM((CELLS, CHANNELS), jnp.float32),
            pltpu.VMEM((CELLS, CHANNELS), jnp.float32),
            pltpu.VMEM((CELLS, KEYS), jnp.float32),
        ]
        + [pltpu.SemaphoreType.DMA] * 8,
        compiler_params=pltpu.CompilerParams(
            collective_id=0, has_side_effects=True, vmem_limit_bytes=48 * 2**20
        ),
    )(
        pole_mask,
        sea_mask,
        queries.reshape(CELLS, CHANNELS),
        key_values.reshape(2, CELLS, CHANNELS),
        reg_queries,
        reg_keys,
    )
    return att.reshape(queries.shape), reg_vals


def solution(mesh):
    return jax.shard_map(
        shards,
        mesh=mesh,
        in_specs=(P("lat", "lon", None), P(None, "lat", "lon", None), P(), P(), P(), P()),
        out_specs=(P("lat", "lon", None), P()),
        check_vma=False,
    )
```

time: 598 us -> 53.2 us (0.09)
  waiting for transfers between devices: 342 us -> 0 us
  blocking collectives: 200 us -> 0 us
  Pallas kernels: 0 us -> 45.9 us
  starting transfers between devices: 23 us -> 0 us
  between operations: 14.4 us -> 0.65 us
    psum x1 -> x0, waiting for transfers between devices: 342 us -> none  [register_values(): lax.psum((weight_sums, weighted), ('lon', 'lat'))]
    psum x1 -> x0, blocking collectives: 100 us -> none  [register_values(): lax.psum((weight_sums, weighted), ('lon', 'lat'))]
    pmax x1 -> x0, blocking collectives: 99.8 us -> none  [register_values(): highest = lax.pmax(jnp.max(scores, axis=2), ('lon', 'lat'))]
    pallas_call x0 -> x1, Pallas kernels: none -> 45.9 us  [shards(): pl.pallas_call(kernel, out_shape=(jax.ShapeDtypeStruct((CELLS, CHANNELS),...]
    ppermute x4 -> x0, starting transfers between devices: 22.9 us -> none  [the longest x2 15.1 us: extended_2(): after = lax.ppermute(leading, axis, down)]
  transfers between devices with their start and end apart: 5 -> 0, of which waited for: 1 -> 0; matrix products, arithmetic and copies ran while one was open for 1% -> 0% of each run, Pallas kernels for 0% -> 0%
where the time goes in v1:
time: 53.2 us; the launch traced here: 52.9 us
  Pallas kernels  45.9 us (86%)
  local copies, waits for them, and re-layouts  6.32 us (12%)
  between operations  0.65 us (1%)
    pallas_call x1, Pallas kernels, shards(): pl.pallas_call(kernel, out_shape=(jax.ShapeDtypeStruct((CELLS, CHANNELS),...  45.9 us
    unnamed x14, local copies, waits for them, and re-layouts  6.32 us

profile of v1, /device:TPU:1, one launch (start us, length us, event | category | flops | bytes accessed | tf_op | source)
XLA Modules:
  0.0 52.9 jit_solution(146907799422484096)
XLA Ops:
  0.6 0.0 copy-start.5
  0.6 0.6 %copy-done.5 = s32[8]{0:T(128)S(1)} copy-done((s32[8]{0:T(128)S(1)}, s32[8]{0:T(128)}, u32[]{:S(2)}) %copy-start.5) | copy-done | bytes 56
  1.3 0.0 copy-start
  1.3 0.9 %copy-done = bf16[2,16,16,256]{3,2,1,0:T(8,128)(2,1)S(1)} copy-done((bf16[2,16,16,256]{3,2,1,0:T(8,128)(2,1)S(1)}, bf16[2,16,16,256]{3,2,1,0:T(8,128)(2,1)}, u32[]{:S(2)}) %copy-start) | copy-done | bytes 262168
  2.2 0.0 copy-start.1
  2.2 0.9 %copy-done.1 = bf16[16,16,256]{2,1,0:T(8,128)(2,1)S(1)} copy-done((bf16[16,16,256]{2,1,0:T(8,128)(2,1)S(1)}, bf16[16,16,256]{2,1,0:T(8,128)(2,1)}, u32[]{:S(2)}) %copy-start.1) | copy-done | bytes 131096
  3.1 0.0 copy-start.2
  3.1 0.9 %copy-done.2 = bf16[256,256]{1,0:T(8,128)(2,1)S(1)} copy-done((bf16[256,256]{1,0:T(8,128)(2,1)S(1)}, bf16[256,256]{1,0:T(8,128)(2,1)}, u32[]{:S(2)}) %copy-start.2) | copy-done | bytes 131096
  4.0 0.0 copy-start.3
  4.0 0.9 %copy-done.3 = bf16[256,256]{1,0:T(8,128)(2,1)S(1)} copy-done((bf16[256,256]{1,0:T(8,128)(2,1)S(1)}, bf16[256,256]{1,0:T(8,128)(2,1)}, u32[]{:S(2)}) %copy-start.3) | copy-done | bytes 131096
  5.0 0.0 copy-start.4
  5.0 0.7 %copy-done.4 = s32[8,256]{1,0:T(8,128)S(1)} copy-done((s32[8,256]{1,0:T(8,128)S(1)}, s32[8,256]{1,0:T(8,128)}, u32[]{:S(2)}) %copy-start.4) | copy-done | bytes 8216
  5.7 45.9 %shard_map.77 = (bf16[256,256]{1,0:T(8,128)(2,1)S(1)}, bf16[256,256]{1,0:T(8,128)(2,1)S(1)}) custom-call(s32[8]{0:T(128)S(1)} %copy-done.5, s32[8,256]{1,0:T(8,128)S(1)} %copy-done.4, bf16[256,256]{1,0:T(8,128)(2,1)S(1)} %bitcast.5, bf16[2,256,256]{2,1,0:T(8,128)(2,1)S(1)} %bitcast.3, bf16[256,256]{1,0:T(8,128)(2,1)S(1)} %copy-done.2, ...), custom_call_target="tpu_custom_call" | custom-call | tf_op jit(solution)/shard_map/pallas_call | solution.py:233
  51.6 0.7 %copy.10 = bf16[16,16,256]{2,1,0:T(8,128)(2,1)} copy(bf16[16,16,256]{2,1,0:T(8,128)(2,1)S(1)} %bitcast.4) | data formatting | bytes 262144
  52.2 0.7 %copy.11 = bf16[256,256]{1,0:T(8,128)(2,1)} copy(bf16[256,256]{1,0:T(8,128)(2,1)S(1)} %get-tuple-element.9) | data formatting | bytes 262144
Async XLA Ops:
  0.6 0.7 %copy-start.5 = (s32[8]{0:T(128)S(1)}, s32[8]{0:T(128)}, u32[]{:S(2)}) copy-start(s32[8]{0:T(128)} %pole.1) | copy-start | bytes 100
  1.3 0.9 %copy-start = (bf16[2,16,16,256]{3,2,1,0:T(8,128)(2,1)S(1)}, bf16[2,16,16,256]{3,2,1,0:T(8,128)(2,1)}, u32[]{:S(2)}) copy-start(bf16[2,16,16,256]{3,2,1,0:T(8,128)(2,1)} %param.7) | copy-start | bytes 786436
  2.2 0.9 %copy-start.1 = (bf16[16,16,256]{2,1,0:T(8,128)(2,1)S(1)}, bf16[16,16,256]{2,1,0:T(8,128)(2,1)}, u32[]{:S(2)}) copy-start(bf16[16,16,256]{2,1,0:T(8,128)(2,1)} %param.6) | copy-start | bytes 393220
  3.1 0.9 %copy-start.2 = (bf16[256,256]{1,0:T(8,128)(2,1)S(1)}, bf16[256,256]{1,0:T(8,128)(2,1)}, u32[]{:S(2)}) copy-start(bf16[256,256]{1,0:T(8,128)(2,1)} %rq.1) | copy-start | bytes 393220
  4.0 0.9 %copy-start.3 = (bf16[256,256]{1,0:T(8,128)(2,1)S(1)}, bf16[256,256]{1,0:T(8,128)(2,1)}, u32[]{:S(2)}) copy-start(bf16[256,256]{1,0:T(8,128)(2,1)} %rk.1) | copy-start | bytes 393220
  5.0 0.7 %copy-start.4 = (s32[8,256]{1,0:T(8,128)S(1)}, s32[8,256]{1,0:T(8,128)}, u32[]{:S(2)}) copy-start(s32[8,256]{1,0:T(8,128)} %sea.1) | copy-start | bytes 24580
